TPU v7x, 256 devices: a whole 4x4x8 slice. The times are simulated.
256 devices in a mesh: slab: 32 (over y_hi, z, core), coil: 8 (over x, y_lo).
Axes of the slice: x: 4, y: 4 (y_hi: 2, y_lo: 2; y = y_hi * 2 + y_lo), z: 8, core: 2. Of those that a mesh axis runs over, the one named last changes fastest.
Arguments:
- image: float32 [2, 128, 128, 256], P(None, 'slab'), may hold values from -6 to 6
- sensitivity: float32 [2, 8, 128, 128, 256], P(None, 'coil', 'slab'), may hold values from -2 to 2
- kspace: float32 [2, 8, 128, 128, 256], P(None, 'coil', None, 'slab'), may hold values from -3 to 3
- sampled: int32 [128, 128], P(None, 'slab'), may hold values 0 or 1
- w_in: bfloat16 [27, 16, 2], replicated, may hold values from -0.875 to 0.875
- w_mid: bfloat16 [27, 16, 16], replicated, may hold values from -0.3125 to 0.3125
- w_out: bfloat16 [27, 2, 16], replicated, may hold values from -0.3125 to 0.3125
Outputs:
- refined: float32 [2, 128, 128, 256], P(None, 'slab', 'coil')
- residual: float32 [2, 8, 128, 128, 256], P(None, 'coil', None, 'slab')
All inputs are finite; a program needn't handle non-finite values. No bound on the sum of `sampled` on one device may be relied on, other than what follows from the above.
Results may differ from a plain program's by a relative error of at most 0.0023.
Values may be sent and summed in bfloat16 or wider, within the bound.
A program may use at most 64 MiB of HBM per device.

v0:
```python
import functools
import math

import jax
import jax.numpy as jnp
import ml_dtypes
import numpy as np
from jax import lax
from jax.experimental import pallas as pl
from jax.experimental.pallas import tpu as pltpu
from jax.sharding import PartitionSpec as P

NX = 256
NY = 128
NZ = 128

step_size = 0.5
SENS_CODE = 16383.0
IMAGE_CODE = 5461.0
DATA_CODE = 3970.0
MESH = pl.DeviceIdType.MESH


def halves(matrix):
    high = matrix.astype(ml_dtypes.bfloat16)
    low = (matrix - high.astype(np.float64)).astype(ml_dtypes.bfloat16)
    return high, low


def blocks(length, inverse):
    positions = np.arange(length)
    angles = (positions[:, None] * positions[None, :] % length) * (2.0 * math.pi / length)
    cosines = np.cos(angles) / math.sqrt(length)
    sines = np.sin(angles) / math.sqrt(length)
    if inverse:
        sines = -sines
    return np.block([[cosines, sines], [-sines, cosines]])


def mixed_rows(matrix):
    return matrix.reshape(2, 32, 4, -1).transpose(1, 0, 2, 3).reshape(256, -1)


def constants():
    forward = blocks(128, False)
    backward = blocks(128, True)
    made = []
    for matrix in (
        mixed_rows(forward.T).T,
        mixed_rows(forward),
        mixed_rows(backward.T).T,
        mixed_rows(backward),
        blocks(256, True),
    ):
        made.extend(halves(matrix))
    return made


def product(pair, data):
    high = data.astype(jnp.bfloat16)
    low = (data - high.astype(jnp.float32)).astype(jnp.bfloat16)
    first, second = (pair[0][...], pair[1][...])
    dot = functools.partial(jnp.dot, preferred_element_type=jnp.float32)
    return dot(first, high) + (dot(first, low) + dot(second, high))


def product_nt(pair, data):
    high = data.astype(jnp.bfloat16)
    low = (data - high.astype(jnp.float32)).astype(jnp.bfloat16)
    first, second = (pair[0][...], pair[1][...])

    def dot(a, b):
        return lax.dot_general(a, b, (((1,), (1,)), ((), ())), preferred_element_type=jnp.float32)

    return dot(first, high) + (dot(first, low) + dot(second, high))


def regrouped(x):
    parts = []
    for k in range(2):
        lanes = slice(128 * k, 128 * k + 128)
        parts.append(jnp.concatenate([x[:128, lanes], x[128:, lanes]], axis=1))
    return jnp.concatenate(parts, axis=0)


def swapped(x):
    return pltpu.roll(x.reshape(32, 8, 128), 4, 1).reshape(256, 128)


def coded(x, scale):
    return jnp.round(x * scale).astype(jnp.int32).astype(jnp.int16)


def companded(x):
    size = jnp.sqrt(jnp.abs(x)) * DATA_CODE
    return jnp.round(jnp.where(x < 0, -size, size)).astype(jnp.int32).astype(jnp.int16)


def decoded(x):
    return x.astype(jnp.int32).astype(jnp.float32)


def gradient_kernel(
    image, sens, kspace, sampled, g1f_h, g1f_l, g2f_h, g2f_l, g1i_h, g1i_l, g2i_h, g2i_l, x_h, x_l,
    current_out, residual_out,
    s_msg, s_rcv, i_msg, i_rcv, y_msg, y_rcv, a_msg, a_rcv, c_msg, c_rcv,
    tmp, sens_a, sens_b, spec, cur, send_sem, recv_sem,
):
    slab = lax.axis_index("slab")
    coil = lax.axis_index("coil")
    me = slab * 8 + coil
    g1f, g2f, g1i, g2i, gx = ((g1f_h, g1f_l), (g2f_h, g2f_l), (g1i_h, g1i_l), (g2i_h, g2i_l), (x_h, x_l))

    def device(p):
        return p // 8, lax.rem(p, 8)

    barrier = pltpu.get_barrier_semaphore()

    def greet(k, _):
        s, c = device(lax.rem(me + k, 256))
        pl.semaphore_signal(barrier, inc=1, device_id={"slab": s, "coil": c}, device_id_type=MESH)
        return 0

    lax.fori_loop(1, 256, greet, 0)

    def send_all(msg, rcv, which):
        def one(k, _):
            s, c = device(lax.rem(me + k, 256))
            pltpu.make_async_remote_copy(
                msg.at[s, c], rcv.at[slab, coil], send_sem.at[which], recv_sem.at[which],
                device_id={"slab": s, "coil": c}, device_id_type=MESH,
            ).start()
            return 0

        lax.fori_loop(1, 256, one, 0)
        rcv[slab, coil] = msg[slab, coil]

    for ri in range(2):
        for z in range(4):
            tmp[:, :, ri * 4 + z, :] = sens[ri, 0, z].T.reshape(32, 8, 128)
    s_msg[...] = coded(tmp[...], SENS_CODE)
    for ri in range(2):
        for z in range(4):
            tmp[:, :, ri * 4 + z, :] = image[ri, z].T.reshape(32, 8, 128)
    rows = lax.broadcasted_iota(jnp.int32, (8, 4), 0)
    columns = lax.broadcasted_iota(jnp.int32, (8, 4), 1)
    pick = (lax.rem(rows, 4) == columns).astype(jnp.float32)
    mask = lax.dot_general(
        pick, sampled[...].astype(jnp.float32), (((1,), (1,)), ((), ())), preferred_element_type=jnp.float32
    )
    own = coded(tmp[:, coil], IMAGE_CODE)
    i_msg[:, 0] = own
    i_msg[:, 1] = jnp.broadcast_to(coded(mask, 1.0)[None], (32, 8, 128))

    pl.semaphore_wait(barrier, 255)

    def send_image(k, _):
        s = lax.rem(slab + k, 32)
        pltpu.make_async_remote_copy(
            i_msg.at[s], i_rcv.at[slab], send_sem.at[0], recv_sem.at[0],
            device_id={"slab": s, "coil": coil}, device_id_type=MESH,
        ).start()
        return 0

    lax.fori_loop(1, 32, send_image, 0)
    i_rcv[slab] = i_msg[slab]
    send_all(s_msg, s_rcv, 1)

    stacked = jnp.concatenate(
        [jnp.concatenate([kspace[0, 0, :, k, :], kspace[1, 0, :, k, :]], axis=1) for k in range(4)], axis=0
    )
    hybrid = product_nt(gx, stacked)
    for ri in range(2):
        for k in range(4):
            tmp[:, :, ri * 4 + k, :] = hybrid[256 * ri : 256 * ri + 256, 128 * k : 128 * k + 128].reshape(32, 8, 128)
    y_msg[...] = companded(tmp[...])
    send_all(y_msg, y_rcv, 2)

    def arrived(flat, which, count):
        part = flat.at[pl.ds(0, count)]
        pltpu.make_async_copy(part, part, recv_sem.at[which]).wait()

    def left(flat, which, count):
        part = flat.at[pl.ds(0, count)]
        pltpu.make_async_copy(part, part, send_sem.at[which]).wait()

    arrived(i_rcv, 0, 31)
    arrived(s_rcv.reshape(256, 8, 128), 1, 255)
    cur[...] = decoded(i_rcv[:, 0]).reshape(256, 128) * (1.0 / IMAGE_CODE)

    lower = lax.broadcasted_iota(jnp.int32, (256, 128), 0) % 8 < 4

    def unpack(c, _):
        both = decoded(s_rcv[:, c]).reshape(256, 128) * (1.0 / SENS_CODE)
        other = swapped(both)
        sens_a[c] = jnp.where(lower, both, other)
        sens_b[c] = jnp.where(lower, -other, both)
        return 0

    lax.fori_loop(0, 8, unpack, 0)

    def forward(p, now, turned):
        c = 2 * p
        v = jnp.concatenate(
            [sens_a[c] * now + sens_b[c] * turned, sens_a[c + 1] * now + sens_b[c + 1] * turned], axis=1
        )
        return product_nt(g2f, regrouped(product(g1f, v)))

    def backward(p, found, weight):
        c = 2 * p
        res = []
        for k in range(2):
            code = decoded(y_rcv[:, c + k]).reshape(256, 128)
            data = code * jnp.abs(code) * (1.0 / DATA_CODE**2)
            res.append(weight * (found[:, 128 * k : 128 * k + 128] - data))
        b = product_nt(g2i, regrouped(product(g1i, jnp.concatenate(res, axis=1))))
        total = None
        for k in range(2):
            part = b[:, 128 * k : 128 * k + 128]
            term = sens_a[c + k] * part - sens_b[c + k] * swapped(part)
            total = term if total is None else total + term
        return total

    now = cur[...]
    turned = swapped(now)

    def ahead(p, _):
        spec[p] = forward(p, now, turned)
        return 0

    lax.fori_loop(0, 4, ahead, 0)
    arrived(y_rcv.reshape(256, 8, 128), 2, 255)
    weight = decoded(i_rcv[:, 1]).reshape(256, 128)
    grad = lax.fori_loop(0, 4, lambda p, g: g + backward(p, spec[p], weight), jnp.zeros((256, 128), jnp.float32))
    now_1 = now - step_size * grad
    turned_1 = swapped(now_1)

    def again(p, g):
        found = forward(p, now_1, turned_1)
        for k in range(2):
            a_msg[:, 2 * p + k] = found[:, 128 * k : 128 * k + 128].reshape(32, 8, 128).astype(jnp.bfloat16)
        return g + backward(p, found, weight)

    grad = lax.fori_loop(0, 4, again, jnp.zeros((256, 128), jnp.float32))
    cur[...] = now_1 - step_size * grad

    lane = lax.broadcasted_iota(jnp.int32, (32, 128), 1) // 16
    picked = [cur[pl.ds(r, 32, stride=8), :] for r in range(8)]
    for c in range(8):
        packed = None
        for r in range(8):
            shift = 16 * ((r - c) % 8)
            moved = pltpu.roll(picked[r], shift, 1) if shift else picked[r]
            packed = moved if packed is None else jnp.where(lane == r, moved, packed)
        c_msg[:, c, 0, :] = packed
    send_all(c_msg, c_rcv, 4)
    send_all(a_msg, a_rcv, 3)

    arrived(c_rcv.reshape(256, 1, 128), 4, 255)
    current_out[...] = c_rcv[:, :, 0, :].reshape(256, 128).T

    arrived(a_rcv.reshape(256, 8, 128), 3, 255)
    tmp[...] = a_rcv[...].astype(jnp.float32)
    keep = sampled[...].astype(jnp.float32)
    for k in range(4):
        parts = [tmp[:, :, 4 * ri + k, :].reshape(256, 128).T.astype(jnp.bfloat16) for ri in range(2)]
        found = jnp.concatenate(parts, axis=1)
        found = jnp.dot(found, x_h[...], preferred_element_type=jnp.float32) + jnp.dot(
            found, x_l[...], preferred_element_type=jnp.float32
        )
        here = keep[:, k : k + 1]
        residual_out[0, 0, :, k, :] = here * (found[:, :256] - kspace[0, 0, :, k, :])
        residual_out[1, 0, :, k, :] = here * (found[:, 256:] - kspace[1, 0, :, k, :])
    left(i_msg, 0, 31)
    left(s_msg.reshape(256, 8, 128), 1, 255)
    left(y_msg.reshape(256, 8, 128), 2, 255)
    left(a_msg.reshape(256, 8, 128), 3, 255)
    left(c_msg.reshape(256, 1, 128), 4, 255)


def gradient_steps(image, sensitivity, kspace, sampled):
    whole = pl.BlockSpec(memory_space=pltpu.VMEM)
    tables = [jnp.asarray(m) for m in constants()]
    small = [pltpu.VMEM((32, 8, 8, 128), jnp.int16) for _ in range(2)]
    return pl.pallas_call(
        gradient_kernel,
        out_shape=(
            jax.ShapeDtypeStruct((128, 256), jnp.float32),
            jax.ShapeDtypeStruct((2, 1, 128, 4, 256), jnp.float32),
        ),
        in_specs=[whole] * (4 + len(tables)),
        out_specs=(whole, whole),
        scratch_shapes=small
        + [pltpu.VMEM((32, 2, 8, 128), jnp.int16) for _ in range(2)]
        + small
        + [pltpu.VMEM((32, 8, 8, 128), jnp.bfloat16) for _ in range(2)]
        + [pltpu.VMEM((32, 8, 1, 128), jnp.float32) for _ in range(2)]
        + [
            pltpu.VMEM((32, 8, 8, 128), jnp.float32),
            pltpu.VMEM((8, 256, 128), jnp.float32),
            pltpu.VMEM((8, 256, 128), jnp.float32),
            pltpu.VMEM((4, 256, 256), jnp.float32),
            pltpu.VMEM((256, 128), jnp.float32),
            pltpu.SemaphoreType.DMA((5,)),
            pltpu.SemaphoreType.DMA((5,)),
        ],
        compiler_params=pltpu.CompilerParams(
            collective_id=0, has_side_effects=True, vmem_limit_bytes=48 * 1024 * 1024
        ),
        name="gradient_steps",
    )(image, sensitivity, kspace, sampled, *tables)


def padded_2(x, sides, width):
    for axis, dim in sides:
        size, length = (lax.axis_size(axis), x.shape[dim])
        up = [(i, (i + 1) % size) for i in range(size - 1)]
        down = [(j, i) for i, j in up]
        last = lax.slice_in_dim(x, length - width, length, axis=dim)
        leading = lax.slice_in_dim(x, 0, width, axis=dim)
        before = lax.ppermute(last, axis, up)
        after = lax.ppermute(leading, axis, down)
        x = jnp.concatenate([before, x, after], axis=dim)
    return x


def conv_layer(padded, weight):
    extent_z = padded.shape[1] - 2
    extent_y = padded.shape[2] - 2
    width = padded.shape[3]
    shifted_left = jnp.pad(padded[:, :, :, : width - 1], ((0, 0), (0, 0), (0, 0), (1, 0)))
    shifted_right = jnp.pad(padded[:, :, :, 1:], ((0, 0), (0, 0), (0, 0), (0, 1)))
    stacked = jnp.concatenate([shifted_left, padded, shifted_right], axis=0)
    summed = None
    for offset_z in range(3):
        for offset_y in range(3):
            tap_block = jnp.concatenate(
                [weight[9 * offset_z + 3 * offset_y + offset_x] for offset_x in range(3)], axis=1
            )
            window = stacked[:, offset_z : offset_z + extent_z, offset_y : offset_y + extent_y, :]
            partial_value = jnp.einsum(
                "oi,izyx->ozyx", tap_block, window, preferred_element_type=jnp.float32
            )
            summed = partial_value if summed is None else summed + partial_value
    return summed


def shards(image, sensitivity, kspace, sampled, w_in, w_mid, w_out):
    slab_depth = image.shape[1]
    row_count = image.shape[2] // lax.axis_size("coil")
    current, residual = gradient_steps(image, sensitivity, kspace, sampled)
    current = current.reshape(2, slab_depth, row_count, NX)
    row_start = lax.axis_index("coil") * row_count
    start = current.astype(jnp.bfloat16)
    grown = padded_2(start, (("slab", 1), ("coil", 2)), 3)
    base_z = lax.axis_index("slab") * slab_depth

    def inside(margin):
        cells_z = base_z - margin + jnp.arange(slab_depth + 2 * margin, dtype=jnp.int32)
        cells_y = row_start - margin + jnp.arange(row_count + 2 * margin, dtype=jnp.int32)
        valid_z = ((cells_z >= 0) & (cells_z < NZ)).astype(jnp.float32)
        valid_y = ((cells_y >= 0) & (cells_y < NY)).astype(jnp.float32)
        return (valid_z[:, None] * valid_y[None, :])[None, :, :, None]

    hidden = (jax.nn.relu(conv_layer(grown, w_in)) * inside(2)).astype(jnp.bfloat16)
    hidden = (jax.nn.relu(conv_layer(hidden, w_mid)) * inside(1)).astype(jnp.bfloat16)
    result = conv_layer(hidden, w_out)
    refined = current + result
    return (refined, residual)


def solution(mesh):
    placed = (
        P(None, "slab", None, None),
        P(None, "coil", "slab", None, None),
        P(None, "coil", None, "slab", None),
        P(None, "slab"),
        P(),
        P(),
        P(),
    )
    return jax.shard_map(
        shards,
        mesh=mesh,
        in_specs=placed,
        out_specs=(P(None, "slab", "coil", None), P(None, "coil", None, "slab", None)),
        check_vma=False,
    )
```

profile of v0, /device:TPU:1, one launch (start us, length us, event | category | flops | bytes accessed | tf_op | source)
XLA Modules:
  0.0 136.6 jit_solution(17178829657535063740)
XLA Ops:
  0.6 0.8 copy.77.sampled
  1.4 1.2 copy-done
  2.6 1.2 copy-done.1
  3.9 1.0 copy-done.2
  4.9 1.0 copy-done.3
  6.0 0.9 copy-done.4
  6.9 0.9 copy-done.5
  7.8 0.9 copy-done.6
  8.7 0.9 copy-done.7
  9.6 0.9 copy-done.8
  10.5 0.9 copy-done.9
  11.4 0.9 copy-done.10
  12.3 0.9 copy-done.11
  13.2 78.8 %gradient_steps.1 = (f32[128,256]{1,0:T(8,128)S(1)}, f32[2,1,128,4,256]{4,3,2,1,0:T(4,128)S(1)}) custom-call(f32[2,4,128,256]{3,2,1,0:T(8,128)S(1)} %copy-done, f32[2,1,4,128,256]{4,3,2,1,0:T(8,128)S(1)} %copy-done.1, f32[2,1,128,4,256]{4,3,2,1,0:T(4,128)} %kspace.1, s32[128,4]{1,0:T(8,128)S(1)} %copy.77.sampled, bf16[256,256]{1,0:T(8,128)(2,1)S(1)} %copy-done.4, ...), custom_call_target="tpu_custom_call" | custom-call | tf_op jit(solution)/shard_map/gradient_steps/pallas_call | solution.py:285
  92.2 2.9 %collective-permute-start = (bf16[2,3,16,256]{3,0,2,1:T(2,128)(2,1)S(1)}, bf16[2,3,16,256]{3,0,2,1:T(2,128)(2,1)S(1)}, u32[]{:S(2)}, u32[]{:S(2)}) collective-permute-start(bf16[2,3,16,256]{3,0,2,1:T(2,128)(2,1)S(1)} %get-tuple-element.72), channel_id=1, source_target_pairs={{0,8},{8,16},{16,24},{24,32},{32,40},{40,48},{48,56},{56,64},{64,7... | collective-permute-start | bytes 147464 | tf_op jit(solution)/shard_map/ppermute | solution.py:321
  95.1 1.9 %collective-permute-start.1 = (bf16[2,3,16,256]{3,0,2,1:T(2,128)(2,1)S(1)}, bf16[2,3,16,256]{3,0,2,1:T(2,128)(2,1)S(1)}, u32[]{:S(2)}, u32[]{:S(2)}) collective-permute-start(bf16[2,3,16,256]{3,0,2,1:T(2,128)(2,1)S(1)} %get-tuple-element.73), channel_id=1, source_target_pairs={{8,0},{16,8},{24,16},{32,24},{40,32},{48,40},{56,48},{64,56},{72,6... | collective-permute-start | bytes 147464 | tf_op jit(solution)/shard_map/ppermute | solution.py:322
  98.2 0.7 slice_reduce_fusion.26
  99.0 1.5 %collective-permute-done.1 = bf16[2,3,16,256]{3,0,2,1:T(2,128)(2,1)S(1)} collective-permute-done((bf16[2,3,16,256]{3,0,2,1:T(2,128)(2,1)S(1)}, bf16[2,3,16,256]{3,0,2,1:T(2,128)(2,1)S(1)}, u32[]{:S(2)}, u32[]{:S(2)}) %collective-permute-start.1) | collective-permute-done | bytes 49184 | tf_op jit(solution)/shard_map/ppermute | solution.py:322
  100.6 3.2 %collective-permute-start.2 = (bf16[2,10,3,256]{3,0,2,1:T(2,128)(2,1)S(1)}, bf16[2,10,3,256]{3,0,2,1:T(2,128)(2,1)S(1)}, u32[]{:S(2)}, u32[]{:S(2)}) collective-permute-start(bf16[2,10,3,256]{3,0,2,1:T(2,128)(2,1)S(1)} %get-tuple-element.43), channel_id=1, source_target_pairs={{0,1},{1,2},{2,3},{3,4},{4,5},{5,6},{6,7},{8,9},{9,10},{10,11},{11... | collective-permute-start | bytes 92168 | tf_op jit(solution)/shard_map/ppermute | solution.py:321
  103.8 1.5 %collective-permute-start.3 = (bf16[2,10,3,256]{3,0,2,1:T(2,128)(2,1)S(1)}, bf16[2,10,3,256]{3,0,2,1:T(2,128)(2,1)S(1)}, u32[]{:S(2)}, u32[]{:S(2)}) collective-permute-start(bf16[2,10,3,256]{3,0,2,1:T(2,128)(2,1)S(1)} %get-tuple-element.44), channel_id=1, source_target_pairs={{1,0},{2,1},{3,2},{4,3},{5,4},{6,5},{7,6},{9,8},{10,9},{11,10},{12... | collective-permute-start | bytes 92168 | tf_op jit(solution)/shard_map/ppermute | solution.py:322
  105.3 0.8 slice_reduce_fusion.25
  106.1 0.6 copy.100
  114.6 0.4 fusion.231
  115.0 1.1 fusion.75
  116.2 0.6 fusion.80
  116.8 0.6 fusion.82
  117.4 0.6 fusion.84
  118.0 0.6 fusion.86
  118.6 0.6 fusion.88
  119.2 0.6 fusion.78
  119.8 0.6 fusion.90
  120.3 0.6 fusion.92
  120.9 1.8 %multiply_convert_fusion = bf16[16,8,20,256]{3,0,2,1:T(8,128)(2,1)S(1)} fusion(f32[16,8,20,256]{3,0,2,1:T(8,128)S(1)} %fusion.78, f32[16,8,20,256]{3,0,2,1:T(8,128)S(1)} %fusion.80, f32[16,8,20,256]{3,0,2,1:T(8,128)S(1)} %fusion.82, f32[16,8,20,256]{3,0,2,1:T(8,128)S(1)} %fusion.84, f32[16,8,20,256]{3,0,2,1:T(8,128)S(1)} %fusion.86, ...), kind=kOutput, calls=%fused_computation.30 | convolution fusion | flops 15073856 | bytes 22943232 | tf_op jit(solution)/shard_map/oi,izyx->ozyx/dot_general | solution.py:341
  122.8 0.6 fusion.229
  123.4 0.9 fusion.4
  124.3 0.6 fusion.12
  124.9 0.6 fusion.14
  125.6 0.6 fusion.16
  126.1 0.6 fusion.18
  126.8 0.6 fusion.10
  127.4 0.6 fusion.20
  128.0 0.6 fusion.8
  128.6 0.6 fusion.22
  129.2 1.0 multiply_convert_fusion.1
  130.7 0.6 fusion.6
  134.4 0.5 fusion.72
  134.9 0.7 copy.134
  135.6 1.0 copy.193
  (117 shorter events, 12.8 us)
Async XLA Ops:
  1.4 1.2 copy-start
  2.6 1.2 copy-start.1
  3.9 1.0 copy-start.2
  4.9 1.0 copy-start.3
  6.0 0.9 copy-start.4
  6.9 0.9 copy-start.5
  7.8 0.9 copy-start.6
  8.7 0.9 copy-start.7
  9.6 0.9 copy-start.8
  10.5 0.9 copy-start.9
  11.4 0.9 copy-start.10
  12.3 0.9 copy-start.11
  13.2 83.8 %copy-start.13 = (bf16[27,16,2]{0,2,1:T(2,128)(2,1)S(1)}, bf16[27,16,2]{0,2,1:T(2,128)(2,1)}, u32[]{:S(2)}) copy-start(bf16[27,16,2]{0,2,1:T(2,128)(2,1)} %param.21) | copy-start | bytes 5188
  13.2 84.2 %copy-start.12 = (bf16[27,16,16]{0,2,1:T(8,128)(2,1)S(1)}, bf16[27,16,16]{0,2,1:T(8,128)(2,1)}, u32[]{:S(2)}) copy-start(bf16[27,16,16]{0,2,1:T(8,128)(2,1)} %param.22) | copy-start | bytes 41476
  92.0 6.2 %copy-start.14 = (bf16[27,2,16]{0,2,1:T(8,128)(2,1)S(1)}, bf16[27,2,16]{0,2,1:T(8,128)(2,1)}, u32[]{:S(2)}) copy-start(bf16[27,2,16]{0,2,1:T(8,128)(2,1)} %param.23) | copy-start | bytes 5188
  92.2 6.8 %collective-permute-start = (bf16[2,3,16,256]{3,0,2,1:T(2,128)(2,1)S(1)}, bf16[2,3,16,256]{3,0,2,1:T(2,128)(2,1)S(1)}, u32[]{:S(2)}, u32[]{:S(2)}) collective-permute-start(bf16[2,3,16,256]{3,0,2,1:T(2,128)(2,1)S(1)} %get-tuple-element.72), channel_id=1, source_target_pairs={{0,8},{8,16},{16,24},{24,32},{32,40},{40,48},{48,56},{56,64},{64,7... | collective-permute-start | bytes 147464 | tf_op jit(solution)/shard_map/ppermute | solution.py:321
  95.1 5.4 %collective-permute-start.1 = (bf16[2,3,16,256]{3,0,2,1:T(2,128)(2,1)S(1)}, bf16[2,3,16,256]{3,0,2,1:T(2,128)(2,1)S(1)}, u32[]{:S(2)}, u32[]{:S(2)}) collective-permute-start(bf16[2,3,16,256]{3,0,2,1:T(2,128)(2,1)S(1)} %get-tuple-element.73), channel_id=1, source_target_pairs={{8,0},{16,8},{24,16},{32,24},{40,32},{48,40},{56,48},{64,56},{72,6... | collective-permute-start | bytes 147464 | tf_op jit(solution)/shard_map/ppermute | solution.py:322
  100.6 13.6 %collective-permute-start.2 = (bf16[2,10,3,256]{3,0,2,1:T(2,128)(2,1)S(1)}, bf16[2,10,3,256]{3,0,2,1:T(2,128)(2,1)S(1)}, u32[]{:S(2)}, u32[]{:S(2)}) collective-permute-start(bf16[2,10,3,256]{3,0,2,1:T(2,128)(2,1)S(1)} %get-tuple-element.43), channel_id=1, source_target_pairs={{0,1},{1,2},{2,3},{3,4},{4,5},{5,6},{6,7},{8,9},{9,10},{10,11},{11... | collective-permute-start | bytes 92168 | tf_op jit(solution)/shard_map/ppermute | solution.py:321
  103.8 10.4 %collective-permute-start.3 = (bf16[2,10,3,256]{3,0,2,1:T(2,128)(2,1)S(1)}, bf16[2,10,3,256]{3,0,2,1:T(2,128)(2,1)S(1)}, u32[]{:S(2)}, u32[]{:S(2)}) collective-permute-start(bf16[2,10,3,256]{3,0,2,1:T(2,128)(2,1)S(1)} %get-tuple-element.44), channel_id=1, source_target_pairs={{1,0},{2,1},{3,2},{4,3},{5,4},{6,5},{7,6},{9,8},{10,9},{11,10},{12... | collective-permute-start | bytes 92168 | tf_op jit(solution)/shard_map/ppermute | solution.py:322
  106.7 9.5 %copy-start.21 = (bf16[1,16,2]{1,2,0:T(2,128)(2,1)S(1)}, bf16[1,16,2]{1,2,0:T(2,128)(2,1)}, u32[]{:S(2)}) copy-start(bf16[1,16,2]{1,2,0:T(2,128)(2,1)} %copy.100) | copy-start | bytes 196
  132.0 1.2 copy-start.20
  132.4 1.2 copy-start.18
  132.4 1.2 copy-start.19
  132.8 1.2 copy-start.15
  132.8 1.2 copy-start.16
  132.8 1.2 copy-start.17
  133.2 1.2 copy-start.22
  133.2 1.2 copy-start.23
  133.2 1.2 copy-start.24
where the time goes:
time: 139 us; the launch traced here: 137 us
  Pallas kernels  78.8 us (57%)
  local copies, waits for them, and re-layouts  26.5 us (19%)
  matrix products  16.1 us (12%)
  starting transfers between devices  9.45 us (7%)
  other arithmetic  3.22 us (2%)
  waiting for transfers between devices  1.55 us (1%)
    pallas_call x1, Pallas kernels, gradient_steps(): pl.pallas_call(gradient_kernel, out_shape=(jax.ShapeDtypeStruct((128, 256...  78.8 us
    unnamed x80, local copies, waits for them, and re-layouts  19.2 us
    dot_general x27, matrix products, conv_layer(): jnp.einsum('oi,izyx->ozyx', tap_block, window, preferred_element_type=jnp...  16.1 us
    ppermute x2, starting transfers between devices, padded_2(): before = lax.ppermute(last, axis, up)  6.06 us
    slice x33, local copies, waits for them, and re-layouts, conv_layer(): weight[9 * offset_z + 3 * offset_y + offset_x]  5.67 us
    ppermute x2, starting transfers between devices, padded_2(): after = lax.ppermute(leading, axis, down)  3.39 us
  transfers between devices with their start and end apart: 4, of which 1 were waited for; matrix products, arithmetic and copies ran while one was open for 8% of the time, Pallas kernels for 0%

commit v1 on v0

--- a/solution.py
+++ b/solution.py
@@ -100,12 +100,27 @@
     return x.astype(jnp.int32).astype(jnp.float32)
 
 
-def gradient_kernel(
-    image, sens, kspace, sampled, g1f_h, g1f_l, g2f_h, g2f_l, g1i_h, g1i_l, g2i_h, g2i_l, x_h, x_l,
-    current_out, residual_out,
-    s_msg, s_rcv, i_msg, i_rcv, y_msg, y_rcv, a_msg, a_rcv, c_msg, c_rcv,
-    tmp, sens_a, sens_b, spec, cur, send_sem, recv_sem,
-):
+def padded_rows(ref, z):
+    return ref[pl.ds(z, 3)].reshape(432, 256)
+
+
+def unrolled_kernel(*refs):
+    count = len(OPERANDS)
+    held = refs[count + 2 : 2 * count + 2]
+    load_sem = refs[2 * count + 2]
+    loads = [pltpu.make_async_copy(refs[k], held[k], load_sem.at[k]) for k in range(count)]
+    for load in loads:
+        load.start()
+    image, sens, kspace, sampled, base_1, weight_2, base_3 = held[:7]
+    g1f_h, g1f_l, g2f_h, g2f_l, g1i_h, g1i_l, g2i_h, g2i_l, x_h, x_l = held[7:]
+    refined_out, residual_out = refs[count : count + 2]
+    (
+        s_msg, s_rcv, i_msg, i_rcv, y_msg, y_rcv, a_msg, a_rcv, c_msg, c_rcv,
+        tmp, sens_a, sens_b, spec, cur,
+        zh_msg, zh_rcv, yh_msg, yh_rcv, ch_msg, ch_rcv,
+        block, grown, wide_0, wide_1, wide_2, toeplitz_1, toeplitz_3, matrix_1, matrix_3,
+        send_sem, recv_sem, halo_send, halo_recv,
+    ) = refs[2 * count + 3 :]
     slab = lax.axis_index("slab")
     coil = lax.axis_index("coil")
     me = slab * 8 + coil
@@ -135,10 +150,13 @@
         lax.fori_loop(1, 256, one, 0)
         rcv[slab, coil] = msg[slab, coil]
 
+    loads[1].wait()
     for ri in range(2):
         for z in range(4):
             tmp[:, :, ri * 4 + z, :] = sens[ri, 0, z].T.reshape(32, 8, 128)
     s_msg[...] = coded(tmp[...], SENS_CODE)
+    loads[0].wait()
+    loads[3].wait()
     for ri in range(2):
         for z in range(4):
             tmp[:, :, ri * 4 + z, :] = image[ri, z].T.reshape(32, 8, 128)
@@ -151,6 +169,27 @@
     own = coded(tmp[:, coil], IMAGE_CODE)
     i_msg[:, 0] = own
     i_msg[:, 1] = jnp.broadcast_to(coded(mask, 1.0)[None], (32, 8, 128))
+
+    for number in (2, *range(4, count)):
+        loads[number].wait()
+    for o in range(16):
+        spread = jnp.broadcast_to(base_1[o : o + 1, :], (24, 512))
+        turned = pltpu.roll(spread, 0, 1, stride=1, stride_axis=0)
+        for part in range(4):
+            toeplitz_1[part, pl.ds(o, 20, stride=16), :] = turned[:20, 128 * part : 128 * part + 128]
+    for part in range(4):
+        matrix_1[:, 128 * part : 128 * part + 128] = toeplitz_1[part].astype(jnp.bfloat16)
+    for y in range(16):
+        turned = pltpu.roll(base_3[...], 48 * y, 1) if y else base_3[...]
+        for part in range(7):
+            toeplitz_3[part, :, y, :] = turned[:, 128 * part : 128 * part + 128]
+    for dz in range(3):
+        for ri in range(2):
+            for part in range(7):
+                matrix_3[dz, 16 * ri : 16 * ri + 16, 128 * part : 128 * part + 128] = toeplitz_3[
+                    part, 2 * dz + ri
+                ].astype(jnp.bfloat16)
+    grown[...] = jnp.zeros((10, 2, 24, 256), jnp.float32)
 
     pl.semaphore_wait(barrier, 255)
 
@@ -254,10 +293,108 @@
             packed = moved if packed is None else jnp.where(lane == r, moved, packed)
         c_msg[:, c, 0, :] = packed
     send_all(c_msg, c_rcv, 4)
+    arrived(c_rcv.reshape(256, 1, 128), 4, 255)
+    block[...] = c_rcv[:, :, 0, :].reshape(256, 128).T
+
+    starts = [[block[64 * ri + 16 * z : 64 * ri + 16 * z + 16, :] for ri in range(2)] for z in range(4)]
+    for z in range(4):
+        for ri in range(2):
+            first = starts[z][ri][:8].astype(jnp.bfloat16)
+            last = starts[z][ri][8:].astype(jnp.bfloat16)
+            yh_msg[0, z, ri] = first
+            yh_msg[1, z, ri] = last
+            for side in range(2):
+                if 0 <= z - side < 3:
+                    zh_msg[side, z - side, ri] = starts[z][ri].astype(jnp.bfloat16)
+                    ch_msg[side, 0, z - side, ri] = first
+                    ch_msg[side, 1, z - side, ri] = last
+
+    halos = []
+    for side in range(2):
+        s = lax.rem(slab + (31 if side == 0 else 1), 32)
+        c = lax.rem(coil + (7 if side == 0 else 1), 8)
+        halos.append((zh_msg.at[side], zh_rcv.at[1 - side], s, coil))
+        halos.append((yh_msg.at[side], yh_rcv.at[1 - side], slab, c))
+        for other in range(2):
+            c = lax.rem(coil + (7 if other == 0 else 1), 8)
+            halos.append((ch_msg.at[side, other], ch_rcv.at[1 - side, 1 - other], s, c))
+    halos = [
+        pltpu.make_async_remote_copy(
+            src, dst, halo_send.at[k], halo_recv.at[k], device_id={"slab": s, "coil": c}, device_id_type=MESH
+        )
+        for k, (src, dst, s, c) in enumerate(halos)
+    ]
+    for halo in halos:
+        halo.start()
     send_all(a_msg, a_rcv, 3)
-
-    arrived(c_rcv.reshape(256, 1, 128), 4, 255)
-    current_out[...] = c_rcv[:, :, 0, :].reshape(256, 128).T
+    for halo in halos:
+        halo.wait()
+
+    lane_x = lax.broadcasted_iota(jnp.int32, (1, 256), 1)
+    not_first = (lane_x > 0).astype(jnp.float32)
+    not_last = (lane_x < 255).astype(jnp.float32)
+
+    def shifted(x):
+        return [pltpu.roll(x, 1, 1) * not_first, x, pltpu.roll(x, 255, 1) * not_last]
+
+    for z in range(10):
+        for ri in range(2):
+            if z < 3:
+                middle, low, high = (zh_rcv[0, z, ri], ch_rcv[0, 0, z, ri], ch_rcv[0, 1, z, ri])
+            elif z < 7:
+                middle, low, high = (starts[z - 3][ri], yh_rcv[0, z - 3, ri], yh_rcv[1, z - 3, ri])
+            else:
+                middle, low, high = (zh_rcv[1, z - 7, ri], ch_rcv[1, 0, z - 7, ri], ch_rcv[1, 1, z - 7, ri])
+            grown[z, ri, 0:3, :] = low.astype(jnp.float32)[5:8]
+            grown[z, ri, 3:19, :] = middle.astype(jnp.float32)
+            grown[z, ri, 19:22, :] = high.astype(jnp.float32)[0:3]
+
+    def valid_rows(rows, each, margin, z, depth):
+        y = lax.broadcasted_iota(jnp.int32, (rows, 1), 0) // each + (16 * coil - margin)
+        deep = z + (4 * slab - depth)
+        good = (y >= 0) & (y < NY) & (deep >= 0) & (deep < NZ)
+        return good.astype(jnp.float32)
+
+    def widen(z, _):
+        keep = valid_rows(24, 1, 3, z, 3)
+        both = [shifted(grown[z, ri] * keep) for ri in range(2)]
+        wide_0[z] = jnp.concatenate([both[ri][dx] for dx in range(3) for ri in range(2)], axis=0).astype(jnp.bfloat16)
+        return 0
+
+    lax.fori_loop(0, 10, widen, 0)
+
+    def layer_1(z, _):
+        hidden = jnp.dot(matrix_1[:, :432], padded_rows(wide_0, z), preferred_element_type=jnp.float32)
+        hidden = jnp.maximum(hidden, 0.0) * valid_rows(320, 16, 2, z, 2)
+        for dx, moved in enumerate(shifted(hidden)):
+            wide_1[z, :, dx] = moved.reshape(20, 16, 256).astype(jnp.bfloat16)
+        return 0
+
+    lax.fori_loop(0, 8, layer_1, 0)
+
+    def layer_2(z, _):
+        for y in range(18):
+            window = wide_1[pl.ds(z, 3), y : y + 3].reshape(432, 256)
+            hidden = jnp.dot(weight_2[...], window, preferred_element_type=jnp.float32)
+            cell = 16 * coil - 1 + y
+            deep = z + 4 * slab - 1
+            good = ((cell >= 0) & (cell < NY) & (deep >= 0) & (deep < NZ)).astype(jnp.float32)
+            hidden = jnp.maximum(hidden, 0.0) * good
+            for dx, moved in enumerate(shifted(hidden)):
+                wide_2[z, y, dx] = moved.astype(jnp.bfloat16)
+        return 0
+
+    lax.fori_loop(0, 6, layer_2, 0)
+
+    for z in range(4):
+        total = None
+        for dz in range(3):
+            part = jnp.dot(
+                matrix_3[dz][:, :864], wide_2[z + dz].reshape(864, 256), preferred_element_type=jnp.float32
+            )
+            total = part if total is None else total + part
+        for ri in range(2):
+            refined_out[ri, z] = block[64 * ri + 16 * z : 64 * ri + 16 * z + 16, :] + total[16 * ri : 16 * ri + 16]
 
     arrived(a_rcv.reshape(256, 8, 128), 3, 255)
     tmp[...] = a_rcv[...].astype(jnp.float32)
@@ -278,95 +415,75 @@
     left(c_msg.reshape(256, 1, 128), 4, 255)
 
 
-def gradient_steps(image, sensitivity, kspace, sampled):
+OPERANDS = (
+    ((2, 4, 128, 256), jnp.float32),
+    ((2, 1, 4, 128, 256), jnp.float32),
+    ((2, 1, 128, 4, 256), jnp.float32),
+    ((128, 4), jnp.int32),
+    ((16, 512), jnp.float32),
+    ((16, 432), jnp.bfloat16),
+    ((8, 896), jnp.float32),
+) + (((256, 256), jnp.bfloat16),) * 8 + (((512, 512), jnp.bfloat16),) * 2
+
+
+def unrolled_step(image, sensitivity, kspace, sampled, w_in, w_mid, w_out):
+    base_1 = w_in.astype(jnp.float32).reshape(3, 3, 3, 16, 2).transpose(3, 0, 2, 4, 1)
+    base_1 = jnp.pad(base_1, ((0, 0),) * 4 + ((0, 21),)).reshape(16, 432)
+    base_1 = jnp.pad(base_1, ((0, 0), (0, 80)))
+    weight_2 = w_mid.transpose(1, 0, 2).reshape(16, 432)
+    base_3 = w_out.astype(jnp.float32).reshape(3, 9, 2, 16).transpose(0, 2, 1, 3).reshape(6, 144)
+    base_3 = jnp.pad(base_3, ((0, 2), (0, 752)))
+    operands = (image, sensitivity, kspace, sampled, base_1, weight_2, base_3)
+    operands += tuple(jnp.asarray(m) for m in constants())
     whole = pl.BlockSpec(memory_space=pltpu.VMEM)
-    tables = [jnp.asarray(m) for m in constants()]
-    small = [pltpu.VMEM((32, 8, 8, 128), jnp.int16) for _ in range(2)]
+    message = (32, 8, 8, 128)
+    vmem = pltpu.VMEM
     return pl.pallas_call(
-        gradient_kernel,
+        unrolled_kernel,
         out_shape=(
-            jax.ShapeDtypeStruct((128, 256), jnp.float32),
+            jax.ShapeDtypeStruct((2, 4, 16, 256), jnp.float32),
             jax.ShapeDtypeStruct((2, 1, 128, 4, 256), jnp.float32),
         ),
-        in_specs=[whole] * (4 + len(tables)),
+        in_specs=[pl.BlockSpec(memory_space=pltpu.HBM)] * len(operands),
         out_specs=(whole, whole),
-        scratch_shapes=small
-        + [pltpu.VMEM((32, 2, 8, 128), jnp.int16) for _ in range(2)]
-        + small
-        + [pltpu.VMEM((32, 8, 8, 128), jnp.bfloat16) for _ in range(2)]
-        + [pltpu.VMEM((32, 8, 1, 128), jnp.float32) for _ in range(2)]
+        scratch_shapes=[vmem(shape, dtype) for shape, dtype in OPERANDS]
+        + [pltpu.SemaphoreType.DMA((len(OPERANDS),))]
+        + [vmem(message, jnp.int16), vmem(message, jnp.int16)]
+        + [vmem((32, 2, 8, 128), jnp.int16), vmem((32, 2, 8, 128), jnp.int16)]
+        + [vmem(message, jnp.int16), vmem(message, jnp.int16)]
+        + [vmem(message, jnp.bfloat16), vmem(message, jnp.bfloat16)]
+        + [vmem((32, 8, 1, 128), jnp.float32), vmem((32, 8, 1, 128), jnp.float32)]
         + [
-            pltpu.VMEM((32, 8, 8, 128), jnp.float32),
-            pltpu.VMEM((8, 256, 128), jnp.float32),
-            pltpu.VMEM((8, 256, 128), jnp.float32),
-            pltpu.VMEM((4, 256, 256), jnp.float32),
-            pltpu.VMEM((256, 128), jnp.float32),
+            vmem(message, jnp.float32),
+            vmem((8, 256, 128), jnp.float32),
+            vmem((8, 256, 128), jnp.float32),
+            vmem((4, 256, 256), jnp.float32),
+            vmem((256, 128), jnp.float32),
+            vmem((2, 3, 2, 16, 256), jnp.bfloat16),
+            vmem((2, 3, 2, 16, 256), jnp.bfloat16),
+            vmem((2, 4, 2, 8, 256), jnp.bfloat16),
+            vmem((2, 4, 2, 8, 256), jnp.bfloat16),
+            vmem((2, 2, 3, 2, 8, 256), jnp.bfloat16),
+            vmem((2, 2, 3, 2, 8, 256), jnp.bfloat16),
+            vmem((128, 256), jnp.float32),
+            vmem((10, 2, 24, 256), jnp.float32),
+            vmem((10, 144, 256), jnp.bfloat16),
+            vmem((8, 20, 3, 16, 256), jnp.bfloat16),
+            vmem((6, 18, 3, 16, 256), jnp.bfloat16),
+            vmem((4, 320, 128), jnp.float32),
+            vmem((7, 8, 16, 128), jnp.float32),
+            vmem((320, 512), jnp.bfloat16),
+            vmem((3, 32, 896), jnp.bfloat16),
             pltpu.SemaphoreType.DMA((5,)),
             pltpu.SemaphoreType.DMA((5,)),
+            pltpu.SemaphoreType.DMA((8,)),
+            pltpu.SemaphoreType.DMA((8,)),
         ],
         compiler_params=pltpu.CompilerParams(
-            collective_id=0, has_side_effects=True, vmem_limit_bytes=48 * 1024 * 1024
+            collective_id=0, has_side_effects=True, vmem_limit_bytes=50 * 1024 * 1024
         ),
-        name="gradient_steps",
-    )(image, sensitivity, kspace, sampled, *tables)
-
-
-def padded_2(x, sides, width):
-    for axis, dim in sides:
-        size, length = (lax.axis_size(axis), x.shape[dim])
-        up = [(i, (i + 1) % size) for i in range(size - 1)]
-        down = [(j, i) for i, j in up]
-        last = lax.slice_in_dim(x, length - width, length, axis=dim)
-        leading = lax.slice_in_dim(x, 0, width, axis=dim)
-        before = lax.ppermute(last, axis, up)
-        after = lax.ppermute(leading, axis, down)
-        x = jnp.concatenate([before, x, after], axis=dim)
-    return x
-
-
-def conv_layer(padded, weight):
-    extent_z = padded.shape[1] - 2
-    extent_y = padded.shape[2] - 2
-    width = padded.shape[3]
-    shifted_left = jnp.pad(padded[:, :, :, : width - 1], ((0, 0), (0, 0), (0, 0), (1, 0)))
-    shifted_right = jnp.pad(padded[:, :, :, 1:], ((0, 0), (0, 0), (0, 0), (0, 1)))
-    stacked = jnp.concatenate([shifted_left, padded, shifted_right], axis=0)
-    summed = None
-    for offset_z in range(3):
-        for offset_y in range(3):
-            tap_block = jnp.concatenate(
-                [weight[9 * offset_z + 3 * offset_y + offset_x] for offset_x in range(3)], axis=1
-            )
-            window = stacked[:, offset_z : offset_z + extent_z, offset_y : offset_y + extent_y, :]
-            partial_value = jnp.einsum(
-                "oi,izyx->ozyx", tap_block, window, preferred_element_type=jnp.float32
-            )
-            summed = partial_value if summed is None else summed + partial_value
-    return summed
-
-
-def shards(image, sensitivity, kspace, sampled, w_in, w_mid, w_out):
-    slab_depth = image.shape[1]
-    row_count = image.shape[2] // lax.axis_size("coil")
-    current, residual = gradient_steps(image, sensitivity, kspace, sampled)
-    current = current.reshape(2, slab_depth, row_count, NX)
-    row_start = lax.axis_index("coil") * row_count
-    start = current.astype(jnp.bfloat16)
-    grown = padded_2(start, (("slab", 1), ("coil", 2)), 3)
-    base_z = lax.axis_index("slab") * slab_depth
-
-    def inside(margin):
-        cells_z = base_z - margin + jnp.arange(slab_depth + 2 * margin, dtype=jnp.int32)
-        cells_y = row_start - margin + jnp.arange(row_count + 2 * margin, dtype=jnp.int32)
-        valid_z = ((cells_z >= 0) & (cells_z < NZ)).astype(jnp.float32)
-        valid_y = ((cells_y >= 0) & (cells_y < NY)).astype(jnp.float32)
-        return (valid_z[:, None] * valid_y[None, :])[None, :, :, None]
-
-    hidden = (jax.nn.relu(conv_layer(grown, w_in)) * inside(2)).astype(jnp.bfloat16)
-    hidden = (jax.nn.relu(conv_layer(hidden, w_mid)) * inside(1)).astype(jnp.bfloat16)
-    result = conv_layer(hidden, w_out)
-    refined = current + result
-    return (refined, residual)
+        name="unrolled_step",
+    )(*operands)
 
 
 def solution(mesh):
@@ -380,7 +497,7 @@
         P(),
     )
     return jax.shard_map(
-        shards,
+        unrolled_step,
         mesh=mesh,
         in_specs=placed,
         out_specs=(P(None, "slab", "coil", None), P(None, "coil", None, "slab", None)),

time: 139 us -> 98.8 us (0.71); the launches traced: 137 us -> 98.5 us
  matrix products: 16.1 us -> 0 us
  local copies, waits for them, and re-layouts: 26.5 us -> 11.4 us
  starting transfers between devices: 9.45 us -> 0 us
  Pallas kernels: 78.8 us -> 86.3 us
  other arithmetic: 3.22 us -> 0.01 us
  waiting for transfers between devices: 1.55 us -> 0 us
    dot_general x27 -> x0, matrix products: 16.1 us -> none  [conv_layer(): jnp.einsum('oi,izyx->ozyx', tap_block, window, preferred_element_type=jnp...]
    ppermute x4 -> x0, starting transfers between devices: 9.45 us -> none  [the longest x2 6.06 us: padded_2(): before = lax.ppermute(last, axis, up)]
    unnamed x80 -> x28, local copies, waits for them, and re-layouts: 19.2 us -> 9.83 us
    pallas_call x1, Pallas kernels: 78.8 us -> 86.3 us  [unrolled_step(): pl.pallas_call(unrolled_kernel, out_shape=(jax.ShapeDtypeStruct((2, 4, 16...]
    slice x37 -> x0, local copies, waits for them, and re-layouts: 7.2 us -> none  [the longest x33 5.67 us: conv_layer(): weight[9 * offset_z + 3 * offset_y + offset_x]]
    concatenate x4 -> x0, other arithmetic: 2.96 us -> none  [the longest x3 2.6 us: conv_layer(): stacked = jnp.concatenate([shifted_left, padded, shifted_right], axis=0)]
    ppermute x4 -> x0, waiting for transfers between devices: 1.55 us -> none  [the longest x2 1.54 us: padded_2(): after = lax.ppermute(leading, axis, down)]
  transfers between devices with their start and end apart: 4 -> 0, of which waited for: 1 -> 0; matrix products, arithmetic and copies ran while one was open for 8% -> 0% of each run, Pallas kernels for 0% -> 0%
where the time goes in v1:
time: 98.8 us; the launch traced here: 98.5 us
  Pallas kernels  86.3 us (87%)
  local copies, waits for them, and re-layouts  11.4 us (12%)
    pallas_call x1, Pallas kernels, unrolled_step(): pl.pallas_call(unrolled_kernel, out_shape=(jax.ShapeDtypeStruct((2, 4, 16...  86.3 us
    unnamed x28, local copies, waits for them, and re-layouts  9.83 us

profile of v1, /device:TPU:1, one launch (start us, length us, event | category | flops | bytes accessed | tf_op | source)
XLA Modules:
  0.0 98.5 jit_solution(2331203645367310172)
XLA Ops:
  0.6 0.0 copy-start
  0.6 0.9 copy.23
  1.5 0.8 copy.26
  2.3 0.1 reshape.27
  2.4 0.2 copy.29
  2.6 0.1 pad.17.clone
  2.7 0.1 reshape.24
  2.8 0.0 copy-start.10
  2.8 0.7 copy-done.10
  3.5 0.0 copy-start.4
  3.5 0.1 copy.28.refs_3_
  3.6 0.0 copy-start.2
  3.6 0.0 copy-start.3
  3.6 1.1 %copy.25 = bf16[16,27,16]{2,1,0:T(8,128)(2,1)S(1)} copy(bf16[16,27,16]{1,2,0:T(8,128)(2,1)} %bitcast.7) | data formatting | bytes 27648 | tf_op jit(solution)/shard_map/transpose | solution.py:433
  4.7 0.2 reshape.25.refs_5_
  4.9 0.0 copy-done
  4.9 0.0 copy-done.4
  4.9 0.0 copy-done.2
  4.9 0.0 copy-done.3
  4.9 0.0 copy-start.1
  4.9 1.0 %copy-done.1 = bf16[512,512]{1,0:T(8,128)(2,1)S(1)} copy-done((bf16[512,512]{1,0:T(8,128)(2,1)S(1)}, bf16[512,512]{1,0:T(8,128)(2,1)}, u32[]{:S(2)}) %copy-start.1) | copy-done | bytes 524312
  6.0 0.0 copy-start.5
  6.0 0.9 copy-done.5
  6.9 0.0 copy-start.6
  6.9 0.9 copy-done.6
  7.8 0.0 copy-start.7
  7.8 0.9 copy-done.7
  8.7 0.0 copy-start.8
  8.7 0.9 copy-done.8
  9.6 0.0 copy-start.9
  9.6 0.9 copy-done.9
  10.5 86.3 %unrolled_step.1 = (f32[2,4,16,256]{3,2,1,0:T(8,128)S(1)}, f32[2,1,128,4,256]{4,3,2,1,0:T(4,128)S(1)}) custom-call(f32[2,4,128,256]{3,2,1,0:T(8,128)} %refs_0_.1, f32[2,1,4,128,256]{4,3,2,1,0:T(8,128)} %refs_1_.1, f32[2,1,128,4,256]{4,3,2,1,0:T(4,128)} %refs_2_.1, s32[128,4]{1,0:T(8,128)S(1)} %copy.28.refs_3_, f32[16,512]{1,0:T(8,128)S(1)} %pad_convert_fusion.refs_4_, ...), custom_call_target="tpu_custom_call" | custom-call | tf_op jit(solution)/shard_map/unrolled_step/pallas_call | solution.py:441
  96.8 0.7 copy.32
  97.5 1.0 copy.33
  (3 shorter events, 0.0 us)
Async XLA Ops:
  0.6 4.2 %copy-start = (bf16[512,512]{1,0:T(8,128)(2,1)S(1)}, bf16[512,512]{1,0:T(8,128)(2,1)}, u32[]{:S(2)}) copy-start(bf16[512,512]{1,0:T(8,128)(2,1)} %constant.33.clone.refs_16_) | copy-start | bytes 1572868
  2.8 0.7 copy-start.10
  3.5 1.4 %copy-start.4 = (bf16[256,256]{1,0:T(8,128)(2,1)S(1)}, bf16[256,256]{1,0:T(8,128)(2,1)}, u32[]{:S(2)}) copy-start(bf16[256,256]{1,0:T(8,128)(2,1)} %constant.29.clone.refs_12_) | copy-start | bytes 393220
  3.6 1.3 %copy-start.2 = (bf16[256,256]{1,0:T(8,128)(2,1)S(1)}, bf16[256,256]{1,0:T(8,128)(2,1)}, u32[]{:S(2)}) copy-start(bf16[256,256]{1,0:T(8,128)(2,1)} %constant.31.clone.refs_14_) | copy-start | bytes 393220
  3.6 1.3 %copy-start.3 = (bf16[256,256]{1,0:T(8,128)(2,1)S(1)}, bf16[256,256]{1,0:T(8,128)(2,1)}, u32[]{:S(2)}) copy-start(bf16[256,256]{1,0:T(8,128)(2,1)} %constant.30.clone.refs_13_) | copy-start | bytes 393220
  4.9 1.0 %copy-start.1 = (bf16[512,512]{1,0:T(8,128)(2,1)S(1)}, bf16[512,512]{1,0:T(8,128)(2,1)}, u32[]{:S(2)}) copy-start(bf16[512,512]{1,0:T(8,128)(2,1)} %constant.32.clone.refs_15_) | copy-start | bytes 1572868
  6.0 0.9 copy-start.5
  6.9 0.9 copy-start.6
  7.8 0.9 copy-start.7
  8.7 0.9 copy-start.8
  9.6 0.9 copy-start.9

commit v2 on v1

--- a/solution.py
+++ b/solution.py
@@ -100,6 +100,10 @@
     return x.astype(jnp.int32).astype(jnp.float32)
 
 
+def wrapped(value, size):
+    return jnp.where(value >= size, value - size, value)
+
+
 def padded_rows(ref, z):
     return ref[pl.ds(z, 3)].reshape(432, 256)
 
@@ -111,44 +115,61 @@
     loads = [pltpu.make_async_copy(refs[k], held[k], load_sem.at[k]) for k in range(count)]
     for load in loads:
         load.start()
-    image, sens, kspace, sampled, base_1, weight_2, base_3 = held[:7]
+    image, sens, kspace, sampled, w_in, w_mid, w_out = held[:7]
     g1f_h, g1f_l, g2f_h, g2f_l, g1i_h, g1i_l, g2i_h, g2i_l, x_h, x_l = held[7:]
     refined_out, residual_out = refs[count : count + 2]
     (
         s_msg, s_rcv, i_msg, i_rcv, y_msg, y_rcv, a_msg, a_rcv, c_msg, c_rcv,
         tmp, sens_a, sens_b, spec, cur,
         zh_msg, zh_rcv, yh_msg, yh_rcv, ch_msg, ch_rcv,
-        block, grown, wide_0, wide_1, wide_2, toeplitz_1, toeplitz_3, matrix_1, matrix_3,
+        block, grown, wide_0, wide_1, wide_2, toeplitz_1, toeplitz_3, matrix_1, matrix_3, base_1, base_3, weight_2,
         send_sem, recv_sem, halo_send, halo_recv,
     ) = refs[2 * count + 3 :]
     slab = lax.axis_index("slab")
     coil = lax.axis_index("coil")
-    me = slab * 8 + coil
     g1f, g2f, g1i, g2i, gx = ((g1f_h, g1f_l), (g2f_h, g2f_l), (g1i_h, g1i_l), (g2i_h, g2i_l), (x_h, x_l))
 
-    def device(p):
-        return p // 8, lax.rem(p, 8)
+    coils = [wrapped(coil + k, 8) for k in (4, 5, 3, 2, 6, 7, 1, 0)]
+
+    def every_other(act, first=0, last=16):
+        def rings(k, _):
+            step = (k + 1) // 2 * (2 * lax.rem(k, 2) - 1)
+            for s in (wrapped(slab + 8 + step, 32), wrapped(slab + 24 + step, 32)):
+                for c in coils:
+                    act(s, c)
+            return 0
+
+        lax.fori_loop(first, min(last, 15), rings, 0)
+        if last == 16:
+            for c in coils:
+                act(wrapped(slab + 16, 32), c)
+            for c in coils[:7]:
+                act(slab, c)
 
     barrier = pltpu.get_barrier_semaphore()
-
-    def greet(k, _):
-        s, c = device(lax.rem(me + k, 256))
-        pl.semaphore_signal(barrier, inc=1, device_id={"slab": s, "coil": c}, device_id_type=MESH)
-        return 0
-
-    lax.fori_loop(1, 256, greet, 0)
-
-    def send_all(msg, rcv, which):
-        def one(k, _):
-            s, c = device(lax.rem(me + k, 256))
-            pltpu.make_async_remote_copy(
+    every_other(
+        lambda s, c: pl.semaphore_signal(barrier, inc=1, device_id={"slab": s, "coil": c}, device_id_type=MESH)
+    )
+
+    def arrived(flat, which, count):
+        part = flat.at[pl.ds(0, count)]
+        pltpu.make_async_copy(part, part, recv_sem.at[which]).wait()
+
+    def left(flat, which, count):
+        part = flat.at[pl.ds(0, count)]
+        pltpu.make_async_copy(part, part, send_sem.at[which]).wait()
+
+    def send_all(msg, rcv, which, first=0, last=16):
+        every_other(
+            lambda s, c: pltpu.make_async_remote_copy(
                 msg.at[s, c], rcv.at[slab, coil], send_sem.at[which], recv_sem.at[which],
                 device_id={"slab": s, "coil": c}, device_id_type=MESH,
-            ).start()
-            return 0
-
-        lax.fori_loop(1, 256, one, 0)
-        rcv[slab, coil] = msg[slab, coil]
+            ).start(),
+            first,
+            last,
+        )
+        if last == 16:
+            rcv[slab, coil] = msg[slab, coil]
 
     loads[1].wait()
     for ri in range(2):
@@ -160,18 +181,28 @@
     for ri in range(2):
         for z in range(4):
             tmp[:, :, ri * 4 + z, :] = image[ri, z].T.reshape(32, 8, 128)
-    rows = lax.broadcasted_iota(jnp.int32, (8, 4), 0)
-    columns = lax.broadcasted_iota(jnp.int32, (8, 4), 1)
-    pick = (lax.rem(rows, 4) == columns).astype(jnp.float32)
-    mask = lax.dot_general(
-        pick, sampled[...].astype(jnp.float32), (((1,), (1,)), ((), ())), preferred_element_type=jnp.float32
-    )
+    mask = sampled[...].astype(jnp.float32)
+    mask = jnp.concatenate([mask, mask], axis=0)
     own = coded(tmp[:, coil], IMAGE_CODE)
     i_msg[:, 0] = own
     i_msg[:, 1] = jnp.broadcast_to(coded(mask, 1.0)[None], (32, 8, 128))
 
     for number in (2, *range(4, count)):
         loads[number].wait()
+    tap = lax.broadcasted_iota(jnp.int32, (27, 512), 0)
+    lane = lax.broadcasted_iota(jnp.int32, (27, 512), 1)
+    tap_z, tap_y, tap_x = (tap // 9, lax.rem(tap // 3, 3), lax.rem(tap, 3))
+
+    def placed(taps, spot):
+        return jnp.dot(taps, (lane == spot).astype(jnp.float32), preferred_element_type=jnp.float32)
+
+    taps_1, taps_2, taps_3 = (w[...].astype(jnp.float32) for w in (w_in, w_mid, w_out))
+    base_1[...] = sum(placed(taps_1[:, ri, :], 144 * tap_z + 24 * (2 * tap_x + ri) + tap_y) for ri in range(2))
+    weight_2[...] = sum(placed(taps_2[:, i, :], 16 * tap + i) for i in range(16)).astype(jnp.bfloat16)
+    spread_3 = sum(placed(taps_3[:, i, :], 16 * tap + i) for i in range(16))
+    base_3[...] = jnp.zeros((8, 896), jnp.float32)
+    for dz in range(3):
+        base_3[2 * dz : 2 * dz + 2, 0:144] = spread_3[:, 144 * dz : 144 * dz + 144]
     for o in range(16):
         spread = jnp.broadcast_to(base_1[o : o + 1, :], (24, 512))
         turned = pltpu.roll(spread, 0, 1, stride=1, stride_axis=0)
@@ -194,7 +225,7 @@
     pl.semaphore_wait(barrier, 255)
 
     def send_image(k, _):
-        s = lax.rem(slab + k, 32)
+        s = wrapped(slab + k, 32)
         pltpu.make_async_remote_copy(
             i_msg.at[s], i_rcv.at[slab], send_sem.at[0], recv_sem.at[0],
             device_id={"slab": s, "coil": coil}, device_id_type=MESH,
@@ -214,14 +245,6 @@
             tmp[:, :, ri * 4 + k, :] = hybrid[256 * ri : 256 * ri + 256, 128 * k : 128 * k + 128].reshape(32, 8, 128)
     y_msg[...] = companded(tmp[...])
     send_all(y_msg, y_rcv, 2)
-
-    def arrived(flat, which, count):
-        part = flat.at[pl.ds(0, count)]
-        pltpu.make_async_copy(part, part, recv_sem.at[which]).wait()
-
-    def left(flat, which, count):
-        part = flat.at[pl.ds(0, count)]
-        pltpu.make_async_copy(part, part, send_sem.at[which]).wait()
 
     arrived(i_rcv, 0, 31)
     arrived(s_rcv.reshape(256, 8, 128), 1, 255)
@@ -283,16 +306,17 @@
     grad = lax.fori_loop(0, 4, again, jnp.zeros((256, 128), jnp.float32))
     cur[...] = now_1 - step_size * grad
 
-    lane = lax.broadcasted_iota(jnp.int32, (32, 128), 1) // 16
+    lane_block = lax.broadcasted_iota(jnp.int32, (32, 128), 1) // 16
     picked = [cur[pl.ds(r, 32, stride=8), :] for r in range(8)]
     for c in range(8):
         packed = None
         for r in range(8):
             shift = 16 * ((r - c) % 8)
             moved = pltpu.roll(picked[r], shift, 1) if shift else picked[r]
-            packed = moved if packed is None else jnp.where(lane == r, moved, packed)
+            packed = moved if packed is None else jnp.where(lane_block == r, moved, packed)
         c_msg[:, c, 0, :] = packed
     send_all(c_msg, c_rcv, 4)
+    send_all(a_msg, a_rcv, 3, 0, 6)
     arrived(c_rcv.reshape(256, 1, 128), 4, 255)
     block[...] = c_rcv[:, :, 0, :].reshape(256, 128).T
 
@@ -326,7 +350,7 @@
     ]
     for halo in halos:
         halo.start()
-    send_all(a_msg, a_rcv, 3)
+    send_all(a_msg, a_rcv, 3, 6, 16)
     for halo in halos:
         halo.wait()
 
@@ -375,7 +399,7 @@
     def layer_2(z, _):
         for y in range(18):
             window = wide_1[pl.ds(z, 3), y : y + 3].reshape(432, 256)
-            hidden = jnp.dot(weight_2[...], window, preferred_element_type=jnp.float32)
+            hidden = jnp.dot(weight_2[:, :432], window, preferred_element_type=jnp.float32)
             cell = 16 * coil - 1 + y
             deep = z + 4 * slab - 1
             good = ((cell >= 0) & (cell < NY) & (deep >= 0) & (deep < NZ)).astype(jnp.float32)
@@ -398,7 +422,11 @@
 
     arrived(a_rcv.reshape(256, 8, 128), 3, 255)
     tmp[...] = a_rcv[...].astype(jnp.float32)
-    keep = sampled[...].astype(jnp.float32)
+    rows = lax.broadcasted_iota(jnp.int32, (128, 128), 0)
+    columns = lax.broadcasted_iota(jnp.int32, (128, 128), 1)
+    keep = lax.dot_general(
+        (rows == columns).astype(jnp.float32), mask, (((1,), (1,)), ((), ())), preferred_element_type=jnp.float32
+    )
     for k in range(4):
         parts = [tmp[:, :, 4 * ri + k, :].reshape(256, 128).T.astype(jnp.bfloat16) for ri in range(2)]
         found = jnp.concatenate(parts, axis=1)
@@ -419,21 +447,17 @@
     ((2, 4, 128, 256), jnp.float32),
     ((2, 1, 4, 128, 256), jnp.float32),
     ((2, 1, 128, 4, 256), jnp.float32),
-    ((128, 4), jnp.int32),
-    ((16, 512), jnp.float32),
-    ((16, 432), jnp.bfloat16),
-    ((8, 896), jnp.float32),
+    ((4, 128), jnp.int32),
+    ((16, 2, 27), jnp.bfloat16),
+    ((16, 16, 27), jnp.bfloat16),
+    ((2, 16, 27), jnp.bfloat16),
 ) + (((256, 256), jnp.bfloat16),) * 8 + (((512, 512), jnp.bfloat16),) * 2
 
 
 def unrolled_step(image, sensitivity, kspace, sampled, w_in, w_mid, w_out):
-    base_1 = w_in.astype(jnp.float32).reshape(3, 3, 3, 16, 2).transpose(3, 0, 2, 4, 1)
-    base_1 = jnp.pad(base_1, ((0, 0),) * 4 + ((0, 21),)).reshape(16, 432)
-    base_1 = jnp.pad(base_1, ((0, 0), (0, 80)))
-    weight_2 = w_mid.transpose(1, 0, 2).reshape(16, 432)
-    base_3 = w_out.astype(jnp.float32).reshape(3, 9, 2, 16).transpose(0, 2, 1, 3).reshape(6, 144)
-    base_3 = jnp.pad(base_3, ((0, 2), (0, 752)))
-    operands = (image, sensitivity, kspace, sampled, base_1, weight_2, base_3)
+    operands = (image, sensitivity, kspace, sampled.T) + tuple(
+        w.transpose(1, 2, 0) for w in (w_in, w_mid, w_out)
+    )
     operands += tuple(jnp.asarray(m) for m in constants())
     whole = pl.BlockSpec(memory_space=pltpu.VMEM)
     message = (32, 8, 8, 128)
@@ -474,16 +498,19 @@
             vmem((7, 8, 16, 128), jnp.float32),
             vmem((320, 512), jnp.bfloat16),
             vmem((3, 32, 896), jnp.bfloat16),
+            vmem((16, 512), jnp.float32),
+            vmem((8, 896), jnp.float32),
+            vmem((16, 512), jnp.bfloat16),
             pltpu.SemaphoreType.DMA((5,)),
             pltpu.SemaphoreType.DMA((5,)),
             pltpu.SemaphoreType.DMA((8,)),
             pltpu.SemaphoreType.DMA((8,)),
         ],
         compiler_params=pltpu.CompilerParams(
-            collective_id=0, has_side_effects=True, vmem_limit_bytes=50 * 1024 * 1024
+            collective_id=0, has_side_effects=True, vmem_limit_bytes=52 * 1024 * 1024
         ),
         name="unrolled_step",
-    )(*operands)
+    )(*(pltpu.with_memory_space_constraint(x, pltpu.HBM) for x in operands))
 
 
 def solution(mesh):

time: 98.8 us -> 82.9 us (0.84)
  local copies, waits for them, and re-layouts: 11.4 us -> 1.63 us
  Pallas kernels: 86.3 us -> 80.5 us
    unnamed x28 -> x2, local copies, waits for them, and re-layouts: 9.83 us -> 1.63 us
    pallas_call x1, Pallas kernels: 86.3 us -> 80.5 us  [unrolled_step(): pl.pallas_call(unrolled_kernel, out_shape=(jax.ShapeDtypeStruct((2, 4, 16...]
    transpose x2 -> x0, local copies, waits for them, and re-layouts: 1.07 us -> none  [the longest x1 1.06 us: unrolled_step(): weight_2 = w_mid.transpose(1, 0, 2).reshape(16, 432)]
where the time goes in v2:
time: 82.9 us; the launch traced here: 82.8 us
  Pallas kernels  80.5 us (97%)
  local copies, waits for them, and re-layouts  1.63 us (2%)
    pallas_call x1, Pallas kernels, unrolled_step(): pl.pallas_call(unrolled_kernel, out_shape=(jax.ShapeDtypeStruct((2, 4, 16...  80.5 us

profile of v2, /device:TPU:1, one launch (start us, length us, event | category | flops | bytes accessed | tf_op | source)
XLA Modules:
  0.0 82.8 jit_solution(13686948917561863117)
XLA Ops:
  0.6 80.5 %unrolled_step.1 = (f32[2,4,16,256]{3,2,1,0:T(8,128)S(1)}, f32[2,1,128,4,256]{4,3,2,1,0:T(4,128)S(1)}) custom-call(f32[2,4,128,256]{3,2,1,0:T(8,128)} %refs_0_.1, f32[2,1,4,128,256]{4,3,2,1,0:T(8,128)} %refs_1_.1, f32[2,1,128,4,256]{4,3,2,1,0:T(4,128)} %refs_2_.1, s32[4,128]{1,0:T(4,128)} %bitcast.7, bf16[16,2,27]{2,1,0:T(2,128)(2,1)} %bitcast.5, ...), custom_call_target="tpu_custom_call" | custom-call | tf_op jit(solution)/shard_map/unrolled_step/pallas_call | solution.py:465
  81.2 0.7 copy.21
  81.8 1.0 %copy.22 = f32[2,1,128,4,256]{4,3,2,1,0:T(4,128)} copy(f32[2,1,128,4,256]{4,3,2,1,0:T(4,128)S(1)} %get-tuple-element.5) | data formatting | bytes 2097152

commit v3 on v2

--- a/solution.py
+++ b/solution.py
@@ -122,7 +122,7 @@
         s_msg, s_rcv, i_msg, i_rcv, y_msg, y_rcv, a_msg, a_rcv, c_msg, c_rcv,
         tmp, sens_a, sens_b, spec, cur,
         zh_msg, zh_rcv, yh_msg, yh_rcv, ch_msg, ch_rcv,
-        block, grown, wide_0, wide_1, wide_2, toeplitz_1, toeplitz_3, matrix_1, matrix_3, base_1, base_3, weight_2,
+        block, grown, wide_0, wide_1, wide_2, toeplitz_1, toeplitz_3, matrix_1, matrix_2, matrix_3, base_3,
         send_sem, recv_sem, halo_send, halo_recv,
     ) = refs[2 * count + 3 :]
     slab = lax.axis_index("slab")
@@ -189,37 +189,49 @@
 
     for number in (2, *range(4, count)):
         loads[number].wait()
-    tap = lax.broadcasted_iota(jnp.int32, (27, 512), 0)
-    lane = lax.broadcasted_iota(jnp.int32, (27, 512), 1)
+    tap = lax.broadcasted_iota(jnp.int32, (27, 1024), 0)
+    lane = lax.broadcasted_iota(jnp.int32, (27, 1024), 1)
     tap_z, tap_y, tap_x = (tap // 9, lax.rem(tap // 3, 3), lax.rem(tap, 3))
 
     def placed(taps, spot):
-        return jnp.dot(taps, (lane == spot).astype(jnp.float32), preferred_element_type=jnp.float32)
+        here = (lane == spot).astype(jnp.float32)[:, : 128 * spot_parts]
+        return jnp.dot(taps, here, preferred_element_type=jnp.float32)
+
+    def in_grid(y):
+        return ((y >= 0) & (y < NY)).astype(jnp.float32)
 
     taps_1, taps_2, taps_3 = (w[...].astype(jnp.float32) for w in (w_in, w_mid, w_out))
-    base_1[...] = sum(placed(taps_1[:, ri, :], 144 * tap_z + 24 * (2 * tap_x + ri) + tap_y) for ri in range(2))
-    weight_2[...] = sum(placed(taps_2[:, i, :], 16 * tap + i) for i in range(16)).astype(jnp.bfloat16)
-    spread_3 = sum(placed(taps_3[:, i, :], 16 * tap + i) for i in range(16))
-    base_3[...] = jnp.zeros((8, 896), jnp.float32)
-    for dz in range(3):
-        base_3[2 * dz : 2 * dz + 2, 0:144] = spread_3[:, 144 * dz : 144 * dz + 144]
+    spot_parts = 4
+    base_1 = sum(placed(taps_1[:, ri, :], 144 * tap_z + 24 * (2 * tap_x + ri) + tap_y) for ri in range(2))
+    good = in_grid(lax.broadcasted_iota(jnp.int32, (24, 1), 0) + (16 * coil - 2))
     for o in range(16):
         spread = jnp.broadcast_to(base_1[o : o + 1, :], (24, 512))
-        turned = pltpu.roll(spread, 0, 1, stride=1, stride_axis=0)
+        turned = pltpu.roll(spread, 0, 1, stride=1, stride_axis=0) * good
         for part in range(4):
             toeplitz_1[part, pl.ds(o, 20, stride=16), :] = turned[:20, 128 * part : 128 * part + 128]
     for part in range(4):
         matrix_1[:, 128 * part : 128 * part + 128] = toeplitz_1[part].astype(jnp.bfloat16)
+    spot_parts = 8
+    for dx in range(3):
+        base_2 = sum(
+            placed(taps_2[:, i, :], jnp.where(tap_x == dx, 320 * tap_z + 16 * tap_y + i, -1)) for i in range(16)
+        )
+        for y in range(18):
+            turned = pltpu.roll(base_2, 16 * y, 1) if y else base_2
+            first = 288 * dx + 16 * y
+            matrix_2[first : first + 16, :] = (turned * in_grid(16 * coil - 1 + y)).astype(jnp.bfloat16)
+    spot_parts = 7
+    for dx in range(3):
+        base_3[2 * dx : 2 * dx + 2, :] = sum(
+            placed(taps_3[:, i, :], jnp.where(tap_x == dx, 288 * tap_z + 16 * tap_y + i, -1)) for i in range(16)
+        )
+    base_3[6:8, :] = jnp.zeros((2, 896), jnp.float32)
     for y in range(16):
-        turned = pltpu.roll(base_3[...], 48 * y, 1) if y else base_3[...]
+        turned = pltpu.roll(base_3[...], 16 * y, 1) if y else base_3[...]
         for part in range(7):
             toeplitz_3[part, :, y, :] = turned[:, 128 * part : 128 * part + 128]
-    for dz in range(3):
-        for ri in range(2):
-            for part in range(7):
-                matrix_3[dz, 16 * ri : 16 * ri + 16, 128 * part : 128 * part + 128] = toeplitz_3[
-                    part, 2 * dz + ri
-                ].astype(jnp.bfloat16)
+    for part in range(7):
+        matrix_3[:, 128 * part : 128 * part + 128] = toeplitz_3[part, 0:6].reshape(96, 128).astype(jnp.bfloat16)
     grown[...] = jnp.zeros((10, 2, 24, 256), jnp.float32)
 
     pl.semaphore_wait(barrier, 255)
@@ -290,20 +302,27 @@
         spec[p] = forward(p, now, turned)
         return 0
 
-    lax.fori_loop(0, 4, ahead, 0)
+    lax.fori_loop(0, 4, ahead, 0, unroll=2)
     arrived(y_rcv.reshape(256, 8, 128), 2, 255)
     weight = decoded(i_rcv[:, 1]).reshape(256, 128)
-    grad = lax.fori_loop(0, 4, lambda p, g: g + backward(p, spec[p], weight), jnp.zeros((256, 128), jnp.float32))
+
+    def add_back(p, g):
+        return g + backward(p, spec[p], weight)
+
+    grad = lax.fori_loop(0, 4, add_back, jnp.zeros((256, 128), jnp.float32), unroll=4)
     now_1 = now - step_size * grad
     turned_1 = swapped(now_1)
 
-    def again(p, g):
+    def again(p, _):
         found = forward(p, now_1, turned_1)
         for k in range(2):
             a_msg[:, 2 * p + k] = found[:, 128 * k : 128 * k + 128].reshape(32, 8, 128).astype(jnp.bfloat16)
-        return g + backward(p, found, weight)
-
-    grad = lax.fori_loop(0, 4, again, jnp.zeros((256, 128), jnp.float32))
+        spec[p] = found
+        return 0
+
+    lax.fori_loop(0, 4, again, 0, unroll=4)
+    send_all(a_msg, a_rcv, 3, 0, 3)
+    grad = lax.fori_loop(0, 4, add_back, jnp.zeros((256, 128), jnp.float32), unroll=4)
     cur[...] = now_1 - step_size * grad
 
     lane_block = lax.broadcasted_iota(jnp.int32, (32, 128), 1) // 16
@@ -316,7 +335,7 @@
             packed = moved if packed is None else jnp.where(lane_block == r, moved, packed)
         c_msg[:, c, 0, :] = packed
     send_all(c_msg, c_rcv, 4)
-    send_all(a_msg, a_rcv, 3, 0, 6)
+    send_all(a_msg, a_rcv, 3, 3, 10)
     arrived(c_rcv.reshape(256, 1, 128), 4, 255)
     block[...] = c_rcv[:, :, 0, :].reshape(256, 128).T
 
@@ -350,7 +369,7 @@
     ]
     for halo in halos:
         halo.start()
-    send_all(a_msg, a_rcv, 3, 6, 16)
+    send_all(a_msg, a_rcv, 3, 10, 16)
     for halo in halos:
         halo.wait()
 
@@ -373,50 +392,46 @@
             grown[z, ri, 3:19, :] = middle.astype(jnp.float32)
             grown[z, ri, 19:22, :] = high.astype(jnp.float32)[0:3]
 
-    def valid_rows(rows, each, margin, z, depth):
-        y = lax.broadcasted_iota(jnp.int32, (rows, 1), 0) // each + (16 * coil - margin)
-        deep = z + (4 * slab - depth)
-        good = (y >= 0) & (y < NY) & (deep >= 0) & (deep < NZ)
-        return good.astype(jnp.float32)
+    def deep(z):
+        return ((z >= 0) & (z < NZ)).astype(jnp.float32)
+
+    good_rows = in_grid(lax.broadcasted_iota(jnp.int32, (24, 1), 0) + (16 * coil - 3))
 
     def widen(z, _):
-        keep = valid_rows(24, 1, 3, z, 3)
+        keep = good_rows * deep(z + 4 * slab - 3)
         both = [shifted(grown[z, ri] * keep) for ri in range(2)]
         wide_0[z] = jnp.concatenate([both[ri][dx] for dx in range(3) for ri in range(2)], axis=0).astype(jnp.bfloat16)
         return 0
 
-    lax.fori_loop(0, 10, widen, 0)
+    lax.fori_loop(0, 10, widen, 0, unroll=2)
 
     def layer_1(z, _):
         hidden = jnp.dot(matrix_1[:, :432], padded_rows(wide_0, z), preferred_element_type=jnp.float32)
-        hidden = jnp.maximum(hidden, 0.0) * valid_rows(320, 16, 2, z, 2)
-        for dx, moved in enumerate(shifted(hidden)):
-            wide_1[z, :, dx] = moved.reshape(20, 16, 256).astype(jnp.bfloat16)
+        wide_1[z] = (jnp.maximum(hidden, 0.0) * deep(z + 4 * slab - 2)).astype(jnp.bfloat16)
         return 0
 
     lax.fori_loop(0, 8, layer_1, 0)
 
+    def summed(taps, rows):
+        return (
+            pltpu.roll(taps[:rows], 1, 1) * not_first
+            + taps[rows : 2 * rows]
+            + pltpu.roll(taps[2 * rows :], 255, 1) * not_last
+        )
+
     def layer_2(z, _):
-        for y in range(18):
-            window = wide_1[pl.ds(z, 3), y : y + 3].reshape(432, 256)
-            hidden = jnp.dot(weight_2[:, :432], window, preferred_element_type=jnp.float32)
-            cell = 16 * coil - 1 + y
-            deep = z + 4 * slab - 1
-            good = ((cell >= 0) & (cell < NY) & (deep >= 0) & (deep < NZ)).astype(jnp.float32)
-            hidden = jnp.maximum(hidden, 0.0) * good
-            for dx, moved in enumerate(shifted(hidden)):
-                wide_2[z, y, dx] = moved.astype(jnp.bfloat16)
+        window = wide_1[pl.ds(z, 3)].reshape(960, 256)
+        taps = jnp.dot(matrix_2[:, :960], window, preferred_element_type=jnp.float32)
+        hidden = jnp.maximum(summed(taps, 288), 0.0) * deep(z + 4 * slab - 1)
+        wide_2[z] = hidden.astype(jnp.bfloat16)
         return 0
 
     lax.fori_loop(0, 6, layer_2, 0)
 
     for z in range(4):
-        total = None
-        for dz in range(3):
-            part = jnp.dot(
-                matrix_3[dz][:, :864], wide_2[z + dz].reshape(864, 256), preferred_element_type=jnp.float32
-            )
-            total = part if total is None else total + part
+        window = wide_2[z : z + 3].reshape(864, 256)
+        taps = jnp.dot(matrix_3[:, :864], window, preferred_element_type=jnp.float32)
+        total = summed(taps, 32)
         for ri in range(2):
             refined_out[ri, z] = block[64 * ri + 16 * z : 64 * ri + 16 * z + 16, :] + total[16 * ri : 16 * ri + 16]
 
@@ -492,15 +507,14 @@
             vmem((128, 256), jnp.float32),
             vmem((10, 2, 24, 256), jnp.float32),
             vmem((10, 144, 256), jnp.bfloat16),
-            vmem((8, 20, 3, 16, 256), jnp.bfloat16),
-            vmem((6, 18, 3, 16, 256), jnp.bfloat16),
+            vmem((8, 320, 256), jnp.bfloat16),
+            vmem((6, 288, 256), jnp.bfloat16),
             vmem((4, 320, 128), jnp.float32),
             vmem((7, 8, 16, 128), jnp.float32),
             vmem((320, 512), jnp.bfloat16),
-            vmem((3, 32, 896), jnp.bfloat16),
-            vmem((16, 512), jnp.float32),
+            vmem((864, 1024), jnp.bfloat16),
+            vmem((96, 896), jnp.bfloat16),
             vmem((8, 896), jnp.float32),
-            vmem((16, 512), jnp.bfloat16),
             pltpu.SemaphoreType.DMA((5,)),
             pltpu.SemaphoreType.DMA((5,)),
             pltpu.SemaphoreType.DMA((8,)),

time: 82.9 us -> 78.4 us (0.946)
  Pallas kernels: 80.5 us -> 76 us
    pallas_call x1, Pallas kernels: 80.5 us -> 76 us  [unrolled_step(): pl.pallas_call(unrolled_kernel, out_shape=(jax.ShapeDtypeStruct((2, 4, 16...]
where the time goes in v3:
time: 78.4 us; the launch traced here: 78.3 us
  Pallas kernels  76 us (97%)
  local copies, waits for them, and re-layouts  1.63 us (2%)
    pallas_call x1, Pallas kernels, unrolled_step(): pl.pallas_call(unrolled_kernel, out_shape=(jax.ShapeDtypeStruct((2, 4, 16...  76 us
    unnamed x2, local copies, waits for them, and re-layouts  1.63 us

profile of v3, /device:TPU:1, one launch (start us, length us, event | category | flops | bytes accessed | tf_op | source)
XLA Modules:
  0.0 78.3 jit_solution(11987841231604755715)
XLA Ops:
  0.6 76.0 %unrolled_step.1 = (f32[2,4,16,256]{3,2,1,0:T(8,128)S(1)}, f32[2,1,128,4,256]{4,3,2,1,0:T(4,128)S(1)}) custom-call(f32[2,4,128,256]{3,2,1,0:T(8,128)} %refs_0_.1, f32[2,1,4,128,256]{4,3,2,1,0:T(8,128)} %refs_1_.1, f32[2,1,128,4,256]{4,3,2,1,0:T(4,128)} %refs_2_.1, s32[4,128]{1,0:T(4,128)} %bitcast.7, bf16[16,2,27]{2,1,0:T(2,128)(2,1)} %bitcast.5, ...), custom_call_target="tpu_custom_call" | custom-call | tf_op jit(solution)/shard_map/unrolled_step/pallas_call | solution.py:480
  76.7 0.7 copy.21
  77.3 1.0 %copy.22 = f32[2,1,128,4,256]{4,3,2,1,0:T(4,128)} copy(f32[2,1,128,4,256]{4,3,2,1,0:T(4,128)S(1)} %get-tuple-element.5) | data formatting | bytes 2097152

commit v4 on v3

--- a/solution.py
+++ b/solution.py
@@ -335,7 +335,7 @@
             packed = moved if packed is None else jnp.where(lane_block == r, moved, packed)
         c_msg[:, c, 0, :] = packed
     send_all(c_msg, c_rcv, 4)
-    send_all(a_msg, a_rcv, 3, 3, 10)
+    send_all(a_msg, a_rcv, 3, 3, 16)
     arrived(c_rcv.reshape(256, 1, 128), 4, 255)
     block[...] = c_rcv[:, :, 0, :].reshape(256, 128).T
 
@@ -369,7 +369,6 @@
     ]
     for halo in halos:
         halo.start()
-    send_all(a_msg, a_rcv, 3, 10, 16)
     for halo in halos:
         halo.wait()
 
@@ -410,7 +409,7 @@
         wide_1[z] = (jnp.maximum(hidden, 0.0) * deep(z + 4 * slab - 2)).astype(jnp.bfloat16)
         return 0
 
-    lax.fori_loop(0, 8, layer_1, 0)
+    lax.fori_loop(0, 8, layer_1, 0, unroll=2)
 
     def summed(taps, rows):
         return (
@@ -426,7 +425,7 @@
         wide_2[z] = hidden.astype(jnp.bfloat16)
         return 0
 
-    lax.fori_loop(0, 6, layer_2, 0)
+    lax.fori_loop(0, 6, layer_2, 0, unroll=2)
 
     for z in range(4):
         window = wide_2[z : z + 3].reshape(864, 256)

time: 78.4 us -> 76.4 us (0.974)
  Pallas kernels: 76 us -> 74.1 us
    pallas_call x1, Pallas kernels: 76 us -> 74.1 us  [unrolled_step(): pl.pallas_call(unrolled_kernel, out_shape=(jax.ShapeDtypeStruct((2, 4, 16...]
where the time goes in v4:
time: 76.4 us
  Pallas kernels  74.1 us (97%)
  local copies, waits for them, and re-layouts  1.63 us (2%)
    pallas_call x1, Pallas kernels, unrolled_step(): pl.pallas_call(unrolled_kernel, out_shape=(jax.ShapeDtypeStruct((2, 4, 16...  74.1 us
    unnamed x2, local copies, waits for them, and re-layouts  1.63 us

profile of v4, /device:TPU:1, one launch (start us, length us, event | category | flops | bytes accessed | tf_op | source)
XLA Modules:
  0.0 76.4 jit_solution(12552051554149757386)
XLA Ops:
  0.6 74.1 %unrolled_step.1 = (f32[2,4,16,256]{3,2,1,0:T(8,128)S(1)}, f32[2,1,128,4,256]{4,3,2,1,0:T(4,128)S(1)}) custom-call(f32[2,4,128,256]{3,2,1,0:T(8,128)} %refs_0_.1, f32[2,1,4,128,256]{4,3,2,1,0:T(8,128)} %refs_1_.1, f32[2,1,128,4,256]{4,3,2,1,0:T(4,128)} %refs_2_.1, s32[4,128]{1,0:T(4,128)} %bitcast.7, bf16[16,2,27]{2,1,0:T(2,128)(2,1)} %bitcast.5, ...), custom_call_target="tpu_custom_call" | custom-call | tf_op jit(solution)/shard_map/unrolled_step/pallas_call | solution.py:479
  74.7 0.7 copy.21
  75.4 1.0 %copy.22 = f32[2,1,128,4,256]{4,3,2,1,0:T(4,128)} copy(f32[2,1,128,4,256]{4,3,2,1,0:T(4,128)S(1)} %get-tuple-element.5) | data formatting | bytes 2097152

commit v5 on v4

--- a/solution.py
+++ b/solution.py
@@ -409,7 +409,7 @@
         wide_1[z] = (jnp.maximum(hidden, 0.0) * deep(z + 4 * slab - 2)).astype(jnp.bfloat16)
         return 0
 
-    lax.fori_loop(0, 8, layer_1, 0, unroll=2)
+    lax.fori_loop(0, 8, layer_1, 0, unroll=4)
 
     def summed(taps, rows):
         return (
@@ -425,7 +425,7 @@
         wide_2[z] = hidden.astype(jnp.bfloat16)
         return 0
 
-    lax.fori_loop(0, 6, layer_2, 0, unroll=2)
+    lax.fori_loop(0, 6, layer_2, 0, unroll=3)
 
     for z in range(4):
         window = wide_2[z : z + 3].reshape(864, 256)
@@ -441,15 +441,21 @@
     keep = lax.dot_general(
         (rows == columns).astype(jnp.float32), mask, (((1,), (1,)), ((), ())), preferred_element_type=jnp.float32
     )
+    parts = [
+        jnp.concatenate(
+            [tmp[:, :, 4 * ri + k, :].reshape(256, 128).T.astype(jnp.bfloat16) for ri in range(2)], axis=1
+        )
+        for k in range(4)
+    ]
+    parts = jnp.concatenate(parts, axis=0)
+    found = jnp.dot(parts, x_h[...], preferred_element_type=jnp.float32) + jnp.dot(
+        parts, x_l[...], preferred_element_type=jnp.float32
+    )
     for k in range(4):
-        parts = [tmp[:, :, 4 * ri + k, :].reshape(256, 128).T.astype(jnp.bfloat16) for ri in range(2)]
-        found = jnp.concatenate(parts, axis=1)
-        found = jnp.dot(found, x_h[...], preferred_element_type=jnp.float32) + jnp.dot(
-            found, x_l[...], preferred_element_type=jnp.float32
-        )
         here = keep[:, k : k + 1]
-        residual_out[0, 0, :, k, :] = here * (found[:, :256] - kspace[0, 0, :, k, :])
-        residual_out[1, 0, :, k, :] = here * (found[:, 256:] - kspace[1, 0, :, k, :])
+        rows = slice(128 * k, 128 * k + 128)
+        residual_out[0, 0, :, k, :] = here * (found[rows, :256] - kspace[0, 0, :, k, :])
+        residual_out[1, 0, :, k, :] = here * (found[rows, 256:] - kspace[1, 0, :, k, :])
     left(i_msg, 0, 31)
     left(s_msg.reshape(256, 8, 128), 1, 255)
     left(y_msg.reshape(256, 8, 128), 2, 255)

time: 76.4 us -> 75.9 us (level)
  no operation moved by 1% of the time
where the time goes in v5:
time: 75.9 us; the launch traced here: 75.8 us
  Pallas kernels  73.6 us (97%)
  local copies, waits for them, and re-layouts  1.63 us (2%)
    pallas_call x1, Pallas kernels, unrolled_step(): pl.pallas_call(unrolled_kernel, out_shape=(jax.ShapeDtypeStruct((2, 4, 16...  73.6 us
    unnamed x2, local copies, waits for them, and re-layouts  1.63 us

profile of v5, /device:TPU:1, one launch (start us, length us, event | category | flops | bytes accessed | tf_op | source)
XLA Modules:
  0.0 75.8 jit_solution(11925761980710992842)
XLA Ops:
  0.6 73.6 %unrolled_step.1 = (f32[2,4,16,256]{3,2,1,0:T(8,128)S(1)}, f32[2,1,128,4,256]{4,3,2,1,0:T(4,128)S(1)}) custom-call(f32[2,4,128,256]{3,2,1,0:T(8,128)} %refs_0_.1, f32[2,1,4,128,256]{4,3,2,1,0:T(8,128)} %refs_1_.1, f32[2,1,128,4,256]{4,3,2,1,0:T(4,128)} %refs_2_.1, s32[4,128]{1,0:T(4,128)} %bitcast.7, bf16[16,2,27]{2,1,0:T(2,128)(2,1)} %bitcast.5, ...), custom_call_target="tpu_custom_call" | custom-call | tf_op jit(solution)/shard_map/unrolled_step/pallas_call | solution.py:485
  74.2 0.7 copy.21
  74.9 1.0 %copy.22 = f32[2,1,128,4,256]{4,3,2,1,0:T(4,128)} copy(f32[2,1,128,4,256]{4,3,2,1,0:T(4,128)S(1)} %get-tuple-element.5) | data formatting | bytes 2097152

commit v6 on v5

--- a/solution.py
+++ b/solution.py
@@ -271,7 +271,7 @@
         sens_b[c] = jnp.where(lower, -other, both)
         return 0
 
-    lax.fori_loop(0, 8, unpack, 0)
+    lax.fori_loop(0, 8, unpack, 0, unroll=4)
 
     def forward(p, now, turned):
         c = 2 * p
@@ -402,7 +402,7 @@
         wide_0[z] = jnp.concatenate([both[ri][dx] for dx in range(3) for ri in range(2)], axis=0).astype(jnp.bfloat16)
         return 0
 
-    lax.fori_loop(0, 10, widen, 0, unroll=2)
+    lax.fori_loop(0, 10, widen, 0, unroll=5)
 
     def layer_1(z, _):
         hidden = jnp.dot(matrix_1[:, :432], padded_rows(wide_0, z), preferred_element_type=jnp.float32)

time: 75.9 us -> 75.7 us (level)
  no operation moved by 1% of the time
where the time goes in v6:
time: 75.7 us; the launch traced here: 75.6 us
  Pallas kernels  73.3 us (97%)
  local copies, waits for them, and re-layouts  1.63 us (2%)
    pallas_call x1, Pallas kernels, unrolled_step(): pl.pallas_call(unrolled_kernel, out_shape=(jax.ShapeDtypeStruct((2, 4, 16...  73.3 us
    unnamed x2, local copies, waits for them, and re-layouts  1.63 us

profile of v6, /device:TPU:1, one launch (start us, length us, event | category | flops | bytes accessed | tf_op | source)
XLA Modules:
  0.0 75.6 jit_solution(16169309915492929439)
XLA Ops:
  0.6 73.3 %unrolled_step.1 = (f32[2,4,16,256]{3,2,1,0:T(8,128)S(1)}, f32[2,1,128,4,256]{4,3,2,1,0:T(4,128)S(1)}) custom-call(f32[2,4,128,256]{3,2,1,0:T(8,128)} %refs_0_.1, f32[2,1,4,128,256]{4,3,2,1,0:T(8,128)} %refs_1_.1, f32[2,1,128,4,256]{4,3,2,1,0:T(4,128)} %refs_2_.1, s32[4,128]{1,0:T(4,128)} %bitcast.7, bf16[16,2,27]{2,1,0:T(2,128)(2,1)} %bitcast.5, ...), custom_call_target="tpu_custom_call" | custom-call | tf_op jit(solution)/shard_map/unrolled_step/pallas_call | solution.py:485
  74.0 0.7 copy.21
  74.6 1.0 %copy.22 = f32[2,1,128,4,256]{4,3,2,1,0:T(4,128)} copy(f32[2,1,128,4,256]{4,3,2,1,0:T(4,128)S(1)} %get-tuple-element.5) | data formatting | bytes 2097152
